TPU v7x, 128 devices: a whole 4x4x4 slice. The times are simulated.
128 devices in a mesh: wide: 32 (over z, y_lo, x), narrow: 4 (over y_hi, core).
Axes of the slice: x: 4, y: 4 (y_hi: 2, y_lo: 2; y = y_hi * 2 + y_lo), z: 4, core: 2. Of those that a mesh axis runs over, the one named last changes fastest.
Arguments:
- hidden: bfloat16 [512, 4, 8192], P('narrow', None, 'wide'), may hold values from -0.1796875 to 0.1796875
- grad_out: bfloat16 [512, 8192], P('narrow', 'wide'), may hold values from -6 to 6
- weight_base: bfloat16 [32768, 8192], P('narrow', 'wide'), may hold values from -0.0625 to 0.0625
- block_scale: bfloat16 [2048, 512], P('narrow', 'wide'), may hold values from 0.25 to 4
Outputs:
- grad_hidden: bfloat16 [512, 4, 8192], P('narrow', None, 'wide')
- grad_weight: bfloat16 [8192, 4, 8192], P('narrow', None, 'wide')
All inputs are finite; a program needn't handle non-finite values.
Results may differ from a plain program's by a relative error of at most 0.0049.
Values may be sent and summed in bfloat16 or wider, within the bound.
No kernel may reach another device: no remote copies, remote signals or barrier semaphores. Data moves between devices by JAX's collectives and lax.ppermute only.
A program may use at most 192 MiB of HBM per device.

v0:
```python
import jax
import jax.numpy as jnp
from jax import lax
from jax.sharding import PartitionSpec as P


def from_everyone(shard, axis):
    length = lax.axis_size(axis)
    return lax.all_to_all(
        jnp.broadcast_to(shard[None], (length, *shard.shape)), axis, 0, 0, tiled=True
    )


def joined_along(parts, dim):
    shape = list(parts.shape[1:])
    shape[dim] *= parts.shape[0]
    return jnp.moveaxis(parts, 0, dim).reshape(shape)


def gathered_copies(shard, axis, dim):
    parts = from_everyone(shard, axis)
    return joined_along(parts, dim)


def apply_scales(values, scales):
    height, breadth = values.shape
    widened = jnp.repeat(scales, 16, axis=1).astype(jnp.float32)
    blocked = values.reshape(height // 16, 16, breadth).astype(jnp.float32)
    blocked = blocked * widened[:, None, :]
    return blocked.reshape(height, breadth).astype(jnp.bfloat16)


def per_device(hidden, grad_out, weight_base, block_scale):
    tokens_here, groups, slice_width = hidden.shape
    row_values, row_scales = (
        lax.all_to_all(weight_base, "wide", split_axis=0, concat_axis=1, tiled=True),
        lax.all_to_all(block_scale, "wide", split_axis=0, concat_axis=1, tiled=True),
    )
    values_all, scales_all = (
        lax.all_gather(row_values, "narrow", axis=0, tiled=True),
        lax.all_gather(row_scales, "narrow", axis=0, tiled=True),
    )
    effective = apply_scales(values_all, scales_all)
    contract_last = (((1,), (1,)), ((), ()))
    incoming = gathered_copies(grad_out, "wide", 1)
    summed = lax.dot_general(incoming, effective, contract_last, preferred_element_type=jnp.float32)
    summed, gathered = (summed, incoming)
    grad_hidden = summed.astype(jnp.bfloat16).reshape(tokens_here, groups, slice_width)
    columns_mine = lax.all_to_all(gathered, "narrow", split_axis=1, concat_axis=0, tiled=True)
    hidden_all = lax.all_gather(
        hidden.reshape(tokens_here, groups * slice_width), "narrow", axis=0, tiled=True
    )
    product = lax.dot_general(
        columns_mine, hidden_all, (((0,), (0,)), ((), ())), preferred_element_type=jnp.float32
    )
    grad_weight = product.astype(jnp.bfloat16).reshape(product.shape[0], groups, slice_width)
    return (grad_hidden, grad_weight)


def solution(mesh):
    return jax.shard_map(
        per_device,
        mesh=mesh,
        in_specs=(
            P("narrow", None, "wide"),
            P("narrow", "wide"),
            P("narrow", "wide"),
            P("narrow", "wide"),
        ),
        out_specs=(P("narrow", None, "wide"), P("narrow", None, "wide")),
        check_vma=False,
    )
```

profile of v0, /device:TPU:1, one launch (start us, length us, event | category | flops | bytes accessed | tf_op | source)
XLA Modules:
  0.0 282.5 jit_solution(4466259191748090938)
XLA Ops:
  7.2 0.0 copy-start
  7.2 10.0 %all-to-all-start = ((bf16[32,256,256]{2,1,0:T(8,128)(2,1)}), bf16[32,256,256]{2,1,0:T(8,128)(2,1)}, u32[]{:S(2)}, u32[]{:S(2)}) async-start(bf16[32,256,256]{2,1,0:T(8,128)(2,1)} %bitcast.33), calls=%async_computation | async-start | bytes 8388608 | tf_op jit(solution)/shard_map/all_to_all | solution.py:36
  17.2 0.0 all-gather.5.cloned.1.call-start
  17.2 0.0 copy-done
  17.2 0.7 copy.34
  18.0 0.0 all-gather.5.cloned.1.call-update
  18.0 0.0 all-gather.3.cloned.1.call-start
  18.1 53.2 %all-to-all-done = bf16[32,256,256]{2,1,0:T(8,128)(2,1)} async-done(((bf16[32,256,256]{2,1,0:T(8,128)(2,1)}), bf16[32,256,256]{2,1,0:T(8,128)(2,1)}, u32[]{:S(2)}, u32[]{:S(2)}) %all-to-all-start) | async-done | bytes 4194336 | tf_op jit(solution)/shard_map/all_to_all | solution.py:36
  71.2 6.5 %copy.23 = bf16[256,32,256]{0,2,1:T(8,128)(2,1)} copy(bf16[256,32,256]{2,0,1:T(8,128)(2,1)} %bitcast.1) | data formatting | bytes 8388608 | tf_op jit(solution)/shard_map/all_to_all | solution.py:36
  77.7 0.0 copy-start.2
  77.7 0.0 copy-start.1
  77.7 0.0 all-gather.3.cloned.1.call-update
  77.8 0.7 copy-done.2
  78.5 0.1 all_to_all.49
  78.6 0.1 copy.36
  78.7 0.7 reshape.41
  79.4 10.3 %all-to-all-start.1 = ((bf16[32,2,128]{2,1,0:T(2,128)(2,1)}), bf16[32,2,128]{2,1,0:T(2,128)(2,1)S(1)}, u32[]{:S(2)}, u32[]{:S(2)}) async-start(bf16[32,2,128]{2,1,0:T(2,128)(2,1)} %reshape.41), calls=%async_computation.1 | async-start | bytes 32768 | tf_op jit(solution)/shard_map/all_to_all | solution.py:37
  89.8 0.0 copy-done.1
  89.8 0.1 copy.29
  89.9 6.9 %all-to-all-done.1 = bf16[32,2,128]{2,1,0:T(2,128)(2,1)S(1)} async-done(((bf16[32,2,128]{2,1,0:T(2,128)(2,1)}), bf16[32,2,128]{2,1,0:T(2,128)(2,1)S(1)}, u32[]{:S(2)}, u32[]{:S(2)}) %all-to-all-start.1) | async-done | bytes 16416 | tf_op jit(solution)/shard_map/all_to_all | solution.py:37
  96.8 0.5 broadcast_in_dim.5
  97.3 33.7 %all_to_all.62 = bf16[32,128,256]{1,2,0:T(8,128)(2,1)} all-to-all(bf16[32,128,256]{1,2,0:T(8,128)(2,1)S(1)} %broadcast_in_dim.5), channel_id=1, replica_groups=mesh['wide'=32,'narrow'=4] {'wide'}, dimensions={0} | all-to-all | bytes 4194304 | tf_op jit(solution)/shard_map/all_to_all | solution.py:9
  131.0 6.6 %all-to-all-start.3 = ((bf16[128,4,2048]{0,2,1:T(8,128)(2,1)}), bf16[128,4,2048]{0,2,1:T(8,128)(2,1)}, u32[]{:S(2)}, u32[]{:S(2)}) async-start(bf16[128,4,2048]{0,2,1:T(8,128)(2,1)} %bitcast.11), calls=%async_computation.3 | async-start | bytes 4194304 | tf_op jit(solution)/shard_map/all_to_all | solution.py:49
  137.7 0.1 reshape.42
  137.8 0.1 copy.33
  137.9 51.1 %all_gather.10 = bf16[64,512]{1,0:T(8,128)(2,1)S(1)} all-gather(bf16[16,512]{1,0:T(8,128)(2,1)S(1)} %copy.33), channel_id=1, replica_groups=mesh['wide'=32,'narrow'=4] {'narrow'}, dimensions={0}, use_global_device_ids=true | all-gather | bytes 81920 | tf_op jit(solution)/shard_map/all_gather | solution.py:41
  189.0 0.1 copy.26
  189.1 2.3 broadcast_in_dim.4
  191.4 3.2 %copy.27 = f32[64,8192]{1,0:T(8,128)S(1)} copy(f32[64,8192]{0,1:T(8,128)} %bitcast.32) | data formatting | bytes 4194304 | tf_op jit(solution)/shard_map/convert_element_type | solution.py:27
  194.6 11.2 %mul.11 = f32[64,16,8192]{2,1,0:T(8,128)} broadcast(f32[64,8192]{1,0:T(8,128)S(1)} %copy.27), dimensions={0,2} | broadcast | bytes 35651584 | tf_op jit(solution)/shard_map/mul | solution.py:29
  205.8 33.5 %copy.28 = f32[1024,8192]{0,1:T(8,128)} copy(f32[1024,8192]{1,0:T(8,128)} %bitcast.30) | data formatting | bytes 67108864 | tf_op jit(solution)/shard_map/mul | solution.py:29
  239.3 0.0 all-to-all-done.3
  239.3 2.9 %copy.30 = bf16[4,128,2048]{2,1,0:T(8,128)(2,1)S(1)} copy(bf16[4,128,2048]{1,2,0:T(8,128)(2,1)} %bitcast.12) | data formatting | bytes 4194304 | tf_op jit(solution)/shard_map/all_to_all | solution.py:49
  242.3 0.0 all-gather.5.cloned.1.call-done
  242.3 5.7 %convolution_convert_fusion = bf16[2048,1024]{0,1:T(8,128)(2,1)} fusion(bf16[512,2048]{1,0:T(8,128)(2,1)S(1)} %bitcast.35, bf16[512,1024]{1,0:T(8,128)(2,1)} %all-gather.5.cloned.1.call-done), kind=kOutput, calls=%fused_computation.2 | convolution fusion | flops 2149580800 | bytes 7340032 | tf_op jit(solution)/shard_map/dot_general | solution.py:53
  248.0 7.4 %copy.32 = bf16[2048,4,256]{2,1,0:T(4,128)(2,1)} copy(bf16[2048,4,256]{0,2,1:T(8,128)(2,1)} %bitcast.34) | data formatting | bytes 8388608
  255.4 0.0 all-gather.3.cloned.1.call-done
  255.4 19.3 %fusion.1 = bf16[1024,128]{1,0:T(8,128)(2,1)S(1)} fusion(bf16[128,8192]{0,1:T(8,128)(2,1)} %bitcast.8, f32[1024,8192]{0,1:T(8,128)} %copy.28, bf16[1024,8192]{0,1:T(8,128)(2,1)} %all-gather.3.cloned.1.call-done), kind=kOutput, calls=%fused_computation.3 | convolution fusion | flops 2172780544 | bytes 52690944 | tf_op jit(solution)/shard_map/dot_general | solution.py:46
  274.7 0.9 copy.31
Async XLA Ops:
  7.2 10.1 %copy-start = (bf16[128,4,256]{2,1,0:T(4,128)(2,1)S(1)}, bf16[128,4,256]{2,1,0:T(4,128)(2,1)}, u32[]{:S(2)}) copy-start(bf16[128,4,256]{2,1,0:T(4,128)(2,1)} %param.4) | copy-start | bytes 786436
  7.2 64.1 %all-to-all-start = ((bf16[32,256,256]{2,1,0:T(8,128)(2,1)}), bf16[32,256,256]{2,1,0:T(8,128)(2,1)}, u32[]{:S(2)}, u32[]{:S(2)}) async-start(bf16[32,256,256]{2,1,0:T(8,128)(2,1)} %bitcast.33), calls=%async_computation | async-start | bytes 8388608 | tf_op jit(solution)/shard_map/all_to_all | solution.py:36
  17.2 225.1 %all-gather.5.cloned.1.call-start = ((), (), s32[]{:S(2)}) async-start(), calls=%async_computation.5 | async-start | bytes 1310720 | tf_op jit(solution)/shard_map/all_gather | solution.py:50
  18.0 237.4 %all-gather.3.cloned.1.call-start = ((), (), s32[]{:S(2)}) async-start(), calls=%async_computation.4 | async-start | bytes 20971520 | tf_op jit(solution)/shard_map/all_gather | solution.py:40
  77.7 0.7 copy-start.2
  77.7 12.0 %copy-start.1 = (bf16[128,256]{1,0:T(8,128)(2,1)S(1)}, bf16[128,256]{1,0:T(8,128)(2,1)}, u32[]{:S(2)}) copy-start(bf16[128,256]{1,0:T(8,128)(2,1)} %param.5) | copy-start | bytes 196612
  79.4 17.4 %all-to-all-start.1 = ((bf16[32,2,128]{2,1,0:T(2,128)(2,1)}), bf16[32,2,128]{2,1,0:T(2,128)(2,1)S(1)}, u32[]{:S(2)}, u32[]{:S(2)}) async-start(bf16[32,2,128]{2,1,0:T(2,128)(2,1)} %reshape.41), calls=%async_computation.1 | async-start | bytes 32768 | tf_op jit(solution)/shard_map/all_to_all | solution.py:37
  131.0 108.3 %all-to-all-start.3 = ((bf16[128,4,2048]{0,2,1:T(8,128)(2,1)}), bf16[128,4,2048]{0,2,1:T(8,128)(2,1)}, u32[]{:S(2)}, u32[]{:S(2)}) async-start(bf16[128,4,2048]{0,2,1:T(8,128)(2,1)} %bitcast.11), calls=%async_computation.3 | async-start | bytes 4194304 | tf_op jit(solution)/shard_map/all_to_all | solution.py:49
Sparse Core Ops, SparseCore 0:
  20.3 52.2 all-gather.4
  77.9 162.2 all-gather.2
where the time goes:
time: 284 us; the launch traced here: 282 us
  blocking collectives  84.9 us (30%)
  local copies, waits for them, and re-layouts  71.2 us (25%)
  waiting for transfers between devices  60.2 us (21%)
  starting transfers between devices  27.1 us (10%)
  matrix products  25 us (9%)
  between operations  14.2 us (5%)
    all_to_all x1, waiting for transfers between devices, per_device(): lax.all_to_all(weight_base, 'wide', split_axis=0, concat_axis=1, tiled=True)  53.2 us
    all_gather x1, blocking collectives, per_device(): lax.all_gather(row_scales, 'narrow', axis=0, tiled=True)  51.1 us
    mul x2, local copies, waits for them, and re-layouts, apply_scales(): blocked = blocked * widened[:, None, :]  44.7 us
    all_to_all x1, blocking collectives, from_everyone(): lax.all_to_all(jnp.broadcast_to(shard[None], (length, *shard.shape)), axi...  33.7 us
    dot_general x1, matrix products, per_device(): lax.dot_general(incoming, effective, contract_last, preferred_element_typ...  19.3 us
    unnamed x12, local copies, waits for them, and re-layouts  10.7 us
    all_to_all x1, starting transfers between devices, per_device(): lax.all_to_all(block_scale, 'wide', split_axis=0, concat_axis=1, tiled=True)  10.3 us
    all_to_all x1, starting transfers between devices, per_device(): lax.all_to_all(weight_base, 'wide', split_axis=0, concat_axis=1, tiled=True)  10 us
  transfers between devices with their start and end apart: 5, of which 2 were waited for; matrix products, arithmetic and copies ran while one was open for 27% of the time, Pallas kernels for 0%

commit v1 on v0

--- a/solution.py
+++ b/solution.py
@@ -38,7 +38,10 @@
     )
     values_all, scales_all = (
         lax.all_gather(row_values, "narrow", axis=0, tiled=True),
-        lax.all_gather(row_scales, "narrow", axis=0, tiled=True),
+        jnp.concatenate(
+            lax.all_to_all(jnp.stack([row_scales] * lax.axis_size("narrow")), "narrow", 0, 0),
+            axis=0,
+        ),
     )
     effective = apply_scales(values_all, scales_all)
     contract_last = (((1,), (1,)), ((), ()))

time: 284 us -> 269 us (0.947)
  blocking collectives: 84.9 us -> 51.2 us
  waiting for transfers between devices: 60.2 us -> 84.4 us
  starting transfers between devices: 27.1 us -> 22 us
    all_gather x1 -> x0, blocking collectives: 51.1 us -> none  [per_device(): lax.all_gather(row_scales, 'narrow', axis=0, tiled=True)]
    all_gather x1, waiting for transfers between devices: 0.01 us -> 25.6 us  [per_device(): lax.all_gather(row_values, 'narrow', axis=0, tiled=True)]
    all_to_all x0 -> x1, blocking collectives: none -> 17.3 us  [per_device(): lax.all_to_all(block_scale, 'wide', split_axis=0, concat_axis=1, tiled=True)]
    all_to_all x1, starting transfers between devices: 10.3 us -> 6.08 us  [per_device(): lax.all_to_all(jnp.stack([row_scales] * lax.axis_size('narrow')), 'narrow...]
  transfers between devices with their start and end apart: 5 -> 5, of which waited for: 2 -> 3; matrix products, arithmetic and copies ran while one was open for 27% -> 28% of each run, Pallas kernels for 0% -> 0%
where the time goes in v1:
time: 269 us; the launch traced here: 268 us
  waiting for transfers between devices  84.4 us (31%)
  local copies, waits for them, and re-layouts  70.9 us (26%)
  blocking collectives  51.2 us (19%)
  matrix products  25 us (9%)
  starting transfers between devices  22 us (8%)
  between operations  14.1 us (5%)
    all_to_all x1, waiting for transfers between devices, per_device(): lax.all_to_all(weight_base, 'wide', split_axis=0, concat_axis=1, tiled=True)  53.2 us
    mul x2, local copies, waits for them, and re-layouts, apply_scales(): blocked = blocked * widened[:, None, :]  44.7 us
    all_to_all x1, blocking collectives, from_everyone(): lax.all_to_all(jnp.broadcast_to(shard[None], (length, *shard.shape)), axi...  33.9 us
    all_gather x1, waiting for transfers between devices, per_device(): lax.all_gather(row_values, 'narrow', axis=0, tiled=True)  25.6 us
    dot_general x1, matrix products, per_device(): lax.dot_general(incoming, effective, contract_last, preferred_element_typ...  19.3 us
    all_to_all x1, blocking collectives, per_device(): lax.all_to_all(block_scale, 'wide', split_axis=0, concat_axis=1, tiled=True)  17.3 us
    unnamed x12, local copies, waits for them, and re-layouts  10.1 us
    all_to_all x1, starting transfers between devices, per_device(): lax.all_to_all(weight_base, 'wide', split_axis=0, concat_axis=1, tiled=True)  10 us
  transfers between devices with their start and end apart: 5, of which 3 were waited for; matrix products, arithmetic and copies ran while one was open for 28% of the time, Pallas kernels for 0%

profile of v1, /device:TPU:1, one launch (start us, length us, event | category | flops | bytes accessed | tf_op | source)
XLA Modules:
  0.0 267.6 jit_solution(6495088383972399284)
XLA Ops:
  7.2 0.0 copy-start
  7.2 10.0 %all-to-all-start = ((bf16[32,256,256]{2,1,0:T(8,128)(2,1)}), bf16[32,256,256]{2,1,0:T(8,128)(2,1)}, u32[]{:S(2)}, u32[]{:S(2)}) async-start(bf16[32,256,256]{2,1,0:T(8,128)(2,1)} %bitcast.36), calls=%async_computation | async-start | bytes 8388608 | tf_op jit(solution)/shard_map/all_to_all | solution.py:36
  17.2 0.0 all-gather.5.cloned.1.call-start
  17.2 0.0 copy-done
  17.2 0.7 copy.34
  18.0 0.0 all-gather.5.cloned.1.call-update
  18.0 0.0 all-gather.3.cloned.1.call-start
  18.1 53.2 %all-to-all-done = bf16[32,256,256]{2,1,0:T(8,128)(2,1)} async-done(((bf16[32,256,256]{2,1,0:T(8,128)(2,1)}), bf16[32,256,256]{2,1,0:T(8,128)(2,1)}, u32[]{:S(2)}, u32[]{:S(2)}) %all-to-all-start) | async-done | bytes 4194336 | tf_op jit(solution)/shard_map/all_to_all | solution.py:36
  71.2 6.5 %copy.23 = bf16[256,32,256]{0,2,1:T(8,128)(2,1)} copy(bf16[256,32,256]{2,0,1:T(8,128)(2,1)} %bitcast.1) | data formatting | bytes 8388608 | tf_op jit(solution)/shard_map/all_to_all | solution.py:36
  77.7 0.0 copy-start.2
  77.7 0.0 copy-start.1
  77.7 0.0 all-gather.3.cloned.1.call-update
  77.8 0.7 copy-done.2
  78.5 0.1 all_to_all.50
  78.6 0.1 copy.36
  78.7 0.1 reshape.48
  78.8 17.3 %all_to_all.64 = bf16[32,2,128]{2,1,0:T(2,128)(2,1)S(1)} all-to-all(bf16[32,2,128]{2,1,0:T(2,128)(2,1)S(1)} %reshape.48), channel_id=1, replica_groups=mesh['wide'=32,'narrow'=4] {'wide'}, dimensions={0} | all-to-all | bytes 32768 | tf_op jit(solution)/shard_map/all_to_all | solution.py:37
  96.1 0.1 reshape.49
  96.2 0.1 copy.33
  96.3 0.7 stack.10
  97.0 6.1 %all-to-all-start.2 = ((bf16[4,16,512]{2,1,0:T(8,128)(2,1)}), bf16[4,16,512]{2,1,0:T(8,128)(2,1)S(1)}, u32[]{:S(2)}, u32[]{:S(2)}) async-start(bf16[4,16,512]{2,1,0:T(8,128)(2,1)} %stack.10), calls=%async_computation.2 | async-start | bytes 131072 | tf_op jit(solution)/shard_map/all_to_all | solution.py:42
  103.0 0.0 copy-done.1
  103.0 0.1 copy.29
  103.1 5.5 %all-to-all-done.2 = bf16[4,16,512]{2,1,0:T(8,128)(2,1)S(1)} async-done(((bf16[4,16,512]{2,1,0:T(8,128)(2,1)}), bf16[4,16,512]{2,1,0:T(8,128)(2,1)S(1)}, u32[]{:S(2)}, u32[]{:S(2)}) %all-to-all-start.2) | async-done | bytes 65568 | tf_op jit(solution)/shard_map/all_to_all | solution.py:42
  108.7 0.5 broadcast_in_dim.5
  109.1 33.9 %all_to_all.65 = bf16[32,128,256]{1,2,0:T(8,128)(2,1)} all-to-all(bf16[32,128,256]{1,2,0:T(8,128)(2,1)S(1)} %broadcast_in_dim.5), channel_id=1, replica_groups=mesh['wide'=32,'narrow'=4] {'wide'}, dimensions={0} | all-to-all | bytes 4194304 | tf_op jit(solution)/shard_map/all_to_all | solution.py:9
  143.0 5.8 %all-to-all-start.4 = ((bf16[128,4,2048]{0,2,1:T(8,128)(2,1)}), bf16[128,4,2048]{0,2,1:T(8,128)(2,1)}, u32[]{:S(2)}, u32[]{:S(2)}) async-start(bf16[128,4,2048]{0,2,1:T(8,128)(2,1)} %bitcast.12), calls=%async_computation.4 | async-start | bytes 4194304 | tf_op jit(solution)/shard_map/all_to_all | solution.py:52
  148.9 0.1 copy.26
  149.0 2.3 broadcast_in_dim.4
  151.3 2.8 %copy.27 = f32[64,8192]{1,0:T(8,128)S(1)} copy(f32[64,8192]{0,1:T(8,128)} %bitcast.35) | data formatting | bytes 4194304 | tf_op jit(solution)/shard_map/convert_element_type | solution.py:27
  154.1 11.2 %mul.11 = f32[64,16,8192]{2,1,0:T(8,128)} broadcast(f32[64,8192]{1,0:T(8,128)S(1)} %copy.27), dimensions={0,2} | broadcast | bytes 35651584 | tf_op jit(solution)/shard_map/mul | solution.py:29
  165.3 33.5 %copy.28 = f32[1024,8192]{0,1:T(8,128)} copy(f32[1024,8192]{1,0:T(8,128)} %bitcast.33) | data formatting | bytes 67108864 | tf_op jit(solution)/shard_map/mul | solution.py:29
  198.8 0.0 all-to-all-done.4
  198.8 2.9 %copy.30 = bf16[4,128,2048]{2,1,0:T(8,128)(2,1)S(1)} copy(bf16[4,128,2048]{1,2,0:T(8,128)(2,1)} %bitcast.13) | data formatting | bytes 4194304 | tf_op jit(solution)/shard_map/all_to_all | solution.py:52
  201.8 0.0 all-gather.5.cloned.1.call-done
  201.8 5.7 %convolution_convert_fusion = bf16[2048,1024]{0,1:T(8,128)(2,1)} fusion(bf16[512,2048]{1,0:T(8,128)(2,1)S(1)} %bitcast.38, bf16[512,1024]{1,0:T(8,128)(2,1)} %all-gather.5.cloned.1.call-done), kind=kOutput, calls=%fused_computation.2 | convolution fusion | flops 2149580800 | bytes 7340032 | tf_op jit(solution)/shard_map/dot_general | solution.py:56
  207.5 7.4 %copy.32 = bf16[2048,4,256]{2,1,0:T(4,128)(2,1)} copy(bf16[2048,4,256]{0,2,1:T(8,128)(2,1)} %bitcast.37) | data formatting | bytes 8388608
  214.9 25.6 %all-gather.3.cloned.1.call-done = bf16[1024,8192]{0,1:T(8,128)(2,1)} async-done(((bf16[256,8192]{0,1:T(8,128)(2,1)}), bf16[1024,8192]{0,1:T(8,128)(2,1)}) %all-gather.3.cloned.1.call-update) | async-done | bytes 16777232 | tf_op jit(solution)/shard_map/all_gather | solution.py:40
  240.6 19.3 %fusion.1 = bf16[1024,128]{1,0:T(8,128)(2,1)S(1)} fusion(bf16[128,8192]{0,1:T(8,128)(2,1)} %bitcast.9, f32[1024,8192]{0,1:T(8,128)} %copy.28, bf16[1024,8192]{0,1:T(8,128)(2,1)} %all-gather.3.cloned.1.call-done), kind=kOutput, calls=%fused_computation.3 | convolution fusion | flops 2172780544 | bytes 52690944 | tf_op jit(solution)/shard_map/dot_general | solution.py:49
  259.9 0.9 copy.31
  (1 shorter events, 0.0 us)
Async XLA Ops:
  7.2 10.1 %copy-start = (bf16[128,4,256]{2,1,0:T(4,128)(2,1)S(1)}, bf16[128,4,256]{2,1,0:T(4,128)(2,1)}, u32[]{:S(2)}) copy-start(bf16[128,4,256]{2,1,0:T(4,128)(2,1)} %param.4) | copy-start | bytes 786436
  7.2 64.1 %all-to-all-start = ((bf16[32,256,256]{2,1,0:T(8,128)(2,1)}), bf16[32,256,256]{2,1,0:T(8,128)(2,1)}, u32[]{:S(2)}, u32[]{:S(2)}) async-start(bf16[32,256,256]{2,1,0:T(8,128)(2,1)} %bitcast.36), calls=%async_computation | async-start | bytes 8388608 | tf_op jit(solution)/shard_map/all_to_all | solution.py:36
  17.2 184.6 %all-gather.5.cloned.1.call-start = ((), (), s32[]{:S(2)}) async-start(), calls=%async_computation.6 | async-start | bytes 1310720 | tf_op jit(solution)/shard_map/all_gather | solution.py:53
  18.0 222.6 %all-gather.3.cloned.1.call-start = ((), (), s32[]{:S(2)}) async-start(), calls=%async_computation.5 | async-start | bytes 20971520 | tf_op jit(solution)/shard_map/all_gather | solution.py:40
  77.7 0.7 copy-start.2
  77.7 25.3 %copy-start.1 = (bf16[128,256]{1,0:T(8,128)(2,1)S(1)}, bf16[128,256]{1,0:T(8,128)(2,1)}, u32[]{:S(2)}) copy-start(bf16[128,256]{1,0:T(8,128)(2,1)} %param.5) | copy-start | bytes 196612
  97.0 11.7 %all-to-all-start.2 = ((bf16[4,16,512]{2,1,0:T(8,128)(2,1)}), bf16[4,16,512]{2,1,0:T(8,128)(2,1)S(1)}, u32[]{:S(2)}, u32[]{:S(2)}) async-start(bf16[4,16,512]{2,1,0:T(8,128)(2,1)} %stack.10), calls=%async_computation.2 | async-start | bytes 131072 | tf_op jit(solution)/shard_map/all_to_all | solution.py:42
  143.0 55.8 %all-to-all-start.4 = ((bf16[128,4,2048]{0,2,1:T(8,128)(2,1)}), bf16[128,4,2048]{0,2,1:T(8,128)(2,1)}, u32[]{:S(2)}, u32[]{:S(2)}) async-start(bf16[128,4,2048]{0,2,1:T(8,128)(2,1)} %bitcast.12), calls=%async_computation.4 | async-start | bytes 4194304 | tf_op jit(solution)/shard_map/all_to_all | solution.py:52
Sparse Core Ops, SparseCore 0:
  20.3 52.2 all-gather.4
  77.9 162.6 all-gather.2
